TPU v7x, 512 devices: a whole 4x4x16 slice. The times are simulated.
512 devices in a mesh: seq: 64 (over x, z_hi, y, core), chan: 8 (over z_lo).
Axes of the slice: x: 4, y: 4, z: 16 (z_hi: 2, z_lo: 8; z = z_hi * 8 + z_lo), core: 2. Of those that a mesh axis runs over, the one named last changes fastest.
Arguments:
- q_proj: float32 [8192, 4096], P('seq', 'chan'), may hold values from -6 to 6
- k_proj: float32 [8192, 4096], P('seq', 'chan'), may hold values from -6 to 6
- v_proj: float32 [8192, 4096], P('seq', 'chan'), may hold values from -6 to 6
- taps: float32 [512, 4, 128], P(('seq', 'chan')), may hold values from -0.25 to 0.25
- skip_bias: float32 [4096], P('chan'), may hold values from -1 to 1
- group_index: int32 [4096], P('chan'), may hold values from 0 to 511
- offsets: int32 [4], replicated, may hold values from 0 to 63
Outputs:
- mixed: float32 [8192, 4096], P('seq', 'chan')
All inputs are finite; a program needn't handle non-finite values.
Results may differ from a plain program's by a relative error of at most 0.000054.
Values sent between devices are 32-bit elements; how exact they have to be, the bound alone decides.
A program may use at most 64 MiB of HBM per device.

v0:
```python
import math

import jax
import jax.numpy as jnp
from jax import lax
from jax.sharding import PartitionSpec as P

precise = lax.Precision.HIGHEST


def shifted(block, axis, distance):
    devices = range(lax.axis_size(axis))
    route = [(i - distance, i) for i in devices if i - distance in devices]
    return lax.ppermute(block, axis, route)


def dft_tables(fft_len):
    positions = jnp.arange(fft_len, dtype=jnp.int32)
    phase_idx = positions[:, None] * positions[None, :] % fft_len
    angles = phase_idx.astype(jnp.float32) * (2.0 * math.pi / fft_len)
    return (jnp.cos(angles), jnp.sin(angles))


def exact_dot(left, right):
    return jnp.dot(left, right, precision=precise, preferred_element_type=jnp.float32)


def convolve(pieces, filt_re, filt_im, cos_out, sin_out):
    spec_re = None
    spec_im = None
    for cos_part, sin_part, block in pieces:
        term_re = exact_dot(cos_part, block)
        term_im = exact_dot(sin_part, block)
        spec_re = term_re if spec_re is None else spec_re + term_re
        spec_im = term_im if spec_im is None else spec_im + term_im
    spec_im = -spec_im
    mix_re = spec_re * filt_re - spec_im * filt_im
    mix_im = spec_re * filt_im + spec_im * filt_re
    return exact_dot(cos_out, mix_re) - exact_dot(sin_out, mix_im)


def local(q_proj, k_proj, v_proj, taps, skip_bias, group_index, offsets):
    gated_in = k_proj * v_proj
    block_len = gated_in.shape[0]
    cosine_tab, sine_tab = dft_tables(2 * block_len)
    cos_scaled = cosine_tab / (2 * block_len)
    sin_scaled = sine_tab / (2 * block_len)
    run_taps = lax.all_gather(taps, "chan", axis=0, tiled=True)
    all_taps = lax.all_gather(run_taps, "seq", axis=0, tiled=True)
    tap_re = jnp.einsum("fm,gkm->fgk", cosine_tab[:, :block_len], all_taps, precision=precise)
    tap_im = -jnp.einsum("fm,gkm->fgk", sine_tab[:, :block_len], all_taps, precision=precise)
    lag_count = offsets.shape[0]
    section_count = (lax.axis_size("seq") - 1).bit_length()
    cos_first = cosine_tab[:, :block_len]
    sin_first = sine_tab[:, :block_len]
    cos_second = cosine_tab[:, block_len:]
    sin_second = sine_tab[:, block_len:]
    convolved = jnp.zeros(gated_in.shape, jnp.float32)
    for lag_index in range(lag_count):
        carried = gated_in
        for bit_index in range(section_count):
            arrived = shifted(carried, "seq", 1 << bit_index)
            carried = jnp.where(offsets[lag_index] // (1 << bit_index) % 2 == 1, arrived, carried)
        earlier = shifted(carried, "seq", 1)
        filt_re = jnp.take(tap_re[:, :, lag_index], group_index, axis=1)
        filt_im = jnp.take(tap_im[:, :, lag_index], group_index, axis=1)
        filt_re, filt_im = (filt_re, filt_im)
        convolved = convolved + convolve(
            ((cos_first, sin_first, earlier), (cos_second, sin_second, carried)),
            filt_re,
            filt_im,
            cos_scaled[block_len:],
            sin_scaled[block_len:],
        )
    return q_proj * (convolved + skip_bias[None, :] * gated_in)


def solution(mesh):
    return jax.shard_map(
        local,
        mesh=mesh,
        in_specs=(
            P("seq", "chan"),
            P("seq", "chan"),
            P("seq", "chan"),
            P(("seq", "chan"), None, None),
            P("chan"),
            P("chan"),
            P(),
        ),
        out_specs=P("seq", "chan"),
        check_vma=False,
    )
```

profile of v0, /device:TPU:1, one launch (start us, length us, event | category | flops | bytes accessed | tf_op | source)
XLA Modules:
  0.0 484.4 jit_solution(13945511676556571744)
XLA Ops:
  6.5 1.1 mul.286
  7.6 4.6 collective-permute-start
  12.2 40.3 %all_gather.6 = f32[8,4,128]{2,1,0:T(4,128)S(1)} all-gather(f32[1,4,128]{2,1,0:T(4,128)} %param.12), channel_id=1, replica_groups=mesh['seq'=64,'chan'=8] {'chan'}, dimensions={0}, use_global_device_ids=true | all-gather | bytes 18432 | tf_op jit(solution)/shard_map/all_gather | solution.py:48
  53.1 1.0 fusion.70
  54.1 1.0 fusion.71
  55.1 1.5 fusion.122
  64.3 0.7 compare_select_fusion
  65.1 3.2 collective-permute-start.7
  69.2 2.9 collective-permute-start.1
  74.6 14.9 %collective-permute-start.13 = (f32[128,512]{1,0:T(8,128)S(1)}, f32[128,512]{1,0:T(8,128)S(1)}, u32[]{:S(2)}, u32[]{:S(2)}) collective-permute-start(f32[128,512]{1,0:T(8,128)S(1)} %get-tuple-element.15), channel_id=1, source_target_pairs={{0,16},{8,24},{16,32},{24,40},{32,48},{40,56},{48,64},{56,72},{64,... | collective-permute-start | bytes 786440 | tf_op jit(solution)/shard_map/ppermute | solution.py:14
  89.5 1.9 collective-permute-start.19
  91.5 3.1 collective-permute-start.8
  94.6 114.7 %collective-permute-start.2 = (f32[128,512]{1,0:T(8,128)S(1)}, f32[128,512]{1,0:T(8,128)S(1)}, u32[]{:S(2)}, u32[]{:S(2)}) collective-permute-start(f32[128,512]{1,0:T(8,128)S(1)} %broadcast_select_fusion.19), channel_id=1, source_target_pairs={{0,32},{8,40},{16,48},{24,56},{32,64},{40,72},{48,80},{56,88},{64,... | collective-permute-start | bytes 786440 | tf_op jit(solution)/shard_map/ppermute | solution.py:14
  209.4 20.0 %collective-permute-start.14 = (f32[128,512]{1,0:T(8,128)S(1)}, f32[128,512]{1,0:T(8,128)S(1)}, u32[]{:S(2)}, u32[]{:S(2)}) collective-permute-start(f32[128,512]{1,0:T(8,128)S(1)} %broadcast_select_fusion.7), channel_id=1, source_target_pairs={{0,32},{8,40},{16,48},{24,56},{32,64},{40,72},{48,80},{56,88},{64,... | collective-permute-start | bytes 786440 | tf_op jit(solution)/shard_map/ppermute | solution.py:14
  229.5 7.8 %collective-permute-start.20 = (f32[128,512]{1,0:T(8,128)S(1)}, f32[128,512]{1,0:T(8,128)S(1)}, u32[]{:S(2)}, u32[]{:S(2)}) collective-permute-start(f32[128,512]{1,0:T(8,128)S(1)} %broadcast_select_fusion.1), channel_id=1, source_target_pairs={{0,32},{8,40},{16,48},{24,56},{32,64},{40,72},{48,80},{56,88},{64,... | collective-permute-start | bytes 786440 | tf_op jit(solution)/shard_map/ppermute | solution.py:14
  237.4 10.2 %collective-permute-start.9 = (f32[128,512]{1,0:T(8,128)S(1)}, f32[128,512]{1,0:T(8,128)S(1)}, u32[]{:S(2)}, u32[]{:S(2)}) collective-permute-start(f32[128,512]{1,0:T(8,128)S(1)} %broadcast_select_fusion.14), channel_id=1, source_target_pairs={{0,64},{8,72},{16,80},{24,88},{32,96},{40,104},{48,112},{56,120},{... | collective-permute-start | bytes 786440 | tf_op jit(solution)/shard_map/ppermute | solution.py:14
  247.7 5.7 %collective-permute-start.3 = (f32[128,512]{1,0:T(8,128)S(1)}, f32[128,512]{1,0:T(8,128)S(1)}, u32[]{:S(2)}, u32[]{:S(2)}) collective-permute-start(f32[128,512]{1,0:T(8,128)S(1)} %broadcast_select_fusion.20), channel_id=1, source_target_pairs={{0,64},{8,72},{16,80},{24,88},{32,96},{40,104},{48,112},{56,120},{... | collective-permute-start | bytes 786440 | tf_op jit(solution)/shard_map/ppermute | solution.py:14
  253.4 3.4 collective-permute-start.15
  256.9 8.9 %collective-permute-start.21 = (f32[128,512]{1,0:T(8,128)S(1)}, f32[128,512]{1,0:T(8,128)S(1)}, u32[]{:S(2)}, u32[]{:S(2)}) collective-permute-start(f32[128,512]{1,0:T(8,128)S(1)} %broadcast_select_fusion.2), channel_id=1, source_target_pairs={{0,64},{8,72},{16,80},{24,88},{32,96},{40,104},{48,112},{56,120},{... | collective-permute-start | bytes 786440 | tf_op jit(solution)/shard_map/ppermute | solution.py:14
  265.9 1.3 collective-permute-start.10
  267.3 1.3 collective-permute-start.4
  268.6 4.2 collective-permute-start.16
  272.9 5.6 %collective-permute-start.22 = (f32[128,512]{1,0:T(8,128)S(1)}, f32[128,512]{1,0:T(8,128)S(1)}, u32[]{:S(2)}, u32[]{:S(2)}) collective-permute-start(f32[128,512]{1,0:T(8,128)S(1)} %broadcast_select_fusion.3), channel_id=1, source_target_pairs={{0,128},{8,136},{16,144},{24,152},{32,160},{40,168},{48,176},{56,1... | collective-permute-start | bytes 786440 | tf_op jit(solution)/shard_map/ppermute | solution.py:14
  278.5 2.3 collective-permute-done.10
  280.9 1.3 collective-permute-start.11
  282.2 4.3 collective-permute-done.4
  286.5 1.3 collective-permute-start.5
  287.8 4.3 collective-permute-done.16
  292.1 1.3 collective-permute-start.17
  293.4 4.4 collective-permute-done.22
  297.8 1.3 collective-permute-start.23
  299.1 4.3 collective-permute-done.11
  303.4 4.3 collective-permute-start.12
  308.3 0.8 collective-permute-done.5
  309.7 4.3 collective-permute-start.6
  315.8 21.8 %collective-permute-start.18 = (f32[128,512]{1,0:T(8,128)S(1)}, f32[128,512]{1,0:T(8,128)S(1)}, u32[]{:S(2)}, u32[]{:S(2)}) collective-permute-start(f32[128,512]{1,0:T(8,128)S(1)} %broadcast_select_fusion.11), channel_id=1, source_target_pairs={{0,8},{8,16},{16,24},{24,32},{32,40},{40,48},{48,56},{56,64},{64,7... | collective-permute-start | bytes 786440 | tf_op jit(solution)/shard_map/ppermute | solution.py:14
  338.8 2.1 collective-permute-start.24
  342.7 1.4 fusion.3
  344.1 1.4 convolution_add_fusion.7
  345.5 1.4 fusion.1
  346.9 1.4 convolution_add_fusion.3
  348.3 1.4 fusion
  349.7 1.4 convolution_add_fusion.1
  351.1 88.3 %all-gather.2.cloned.1.call-done = f32[512,4,128]{2,0,1:T(8,128)} async-done(((f32[8,4,128]{2,0,1:T(8,128)}), f32[512,4,128]{2,0,1:T(8,128)}) %all-gather.2.cloned.1.call-update) | async-done | bytes 1048592 | tf_op jit(solution)/shard_map/all_gather | solution.py:49
  439.3 3.0 convolution_negate_fusion
  442.4 1.2 slice_bitcast_fusion
  443.8 2.5 gather_fusion.3
  446.3 1.2 copy.33
  447.5 1.8 fusion.68
  449.3 1.2 slice_bitcast_fusion.1
  450.7 1.6 gather_fusion.2
  453.0 1.2 convolution_subtract_fusion.2
  454.5 1.6 gather_fusion.1
  456.5 1.6 gather_fusion
  458.5 1.6 gather_fusion.5
  460.5 1.6 gather_fusion.4
  462.1 1.0 copy.35
  463.1 1.2 copy.40
  464.3 1.6 gather_fusion.7
  466.1 1.2 copy.38
  467.4 2.3 gather_fusion.6
  469.6 1.2 copy.39
  470.9 1.8 fusion.25
  476.3 1.2 fusion.8
  (103 shorter events, 13.5 us)
Async XLA Ops:
  6.5 62.6 %copy-start.14 = (s32[512]{0:T(512)S(1)}, s32[512]{0:T(512)}, u32[]{:S(2)}) copy-start(s32[512]{0:T(512)} %param.14) | copy-start | bytes 6148
  6.5 432.8 %all-gather.2.cloned.1.call-start = ((), (), s32[]{:S(2)}) async-start(), calls=%async_computation | async-start | bytes 1064960 | tf_op jit(solution)/shard_map/all_gather | solution.py:49
  7.6 57.4 %collective-permute-start = (f32[128,512]{1,0:T(8,128)S(1)}, f32[128,512]{1,0:T(8,128)S(1)}, u32[]{:S(2)}, u32[]{:S(2)}) collective-permute-start(f32[128,512]{1,0:T(8,128)S(1)} %mul.286), channel_id=1, source_target_pairs={{0,8},{8,16},{16,24},{24,32},{32,40},{40,48},{48,56},{56,64},{64,7... | collective-permute-start | bytes 786440 | tf_op jit(solution)/shard_map/ppermute | solution.py:14
  65.1 26.3 %collective-permute-start.7 = (f32[128,512]{1,0:T(8,128)S(1)}, f32[128,512]{1,0:T(8,128)S(1)}, u32[]{:S(2)}, u32[]{:S(2)}) collective-permute-start(f32[128,512]{1,0:T(8,128)S(1)} %get-tuple-element.16), channel_id=1, source_target_pairs={{0,16},{8,24},{16,32},{24,40},{32,48},{40,56},{48,64},{56,72},{64,... | collective-permute-start | bytes 786440 | tf_op jit(solution)/shard_map/ppermute | solution.py:14
  69.2 25.4 %collective-permute-start.1 = (f32[128,512]{1,0:T(8,128)S(1)}, f32[128,512]{1,0:T(8,128)S(1)}, u32[]{:S(2)}, u32[]{:S(2)}) collective-permute-start(f32[128,512]{1,0:T(8,128)S(1)} %get-tuple-element.17), channel_id=1, source_target_pairs={{0,16},{8,24},{16,32},{24,40},{32,48},{40,56},{48,64},{56,72},{64,... | collective-permute-start | bytes 786440 | tf_op jit(solution)/shard_map/ppermute | solution.py:14
  74.6 134.7 %collective-permute-start.13 = (f32[128,512]{1,0:T(8,128)S(1)}, f32[128,512]{1,0:T(8,128)S(1)}, u32[]{:S(2)}, u32[]{:S(2)}) collective-permute-start(f32[128,512]{1,0:T(8,128)S(1)} %get-tuple-element.15), channel_id=1, source_target_pairs={{0,16},{8,24},{16,32},{24,40},{32,48},{40,56},{48,64},{56,72},{64,... | collective-permute-start | bytes 786440 | tf_op jit(solution)/shard_map/ppermute | solution.py:14
  89.5 140.0 %collective-permute-start.19 = (f32[128,512]{1,0:T(8,128)S(1)}, f32[128,512]{1,0:T(8,128)S(1)}, u32[]{:S(2)}, u32[]{:S(2)}) collective-permute-start(f32[128,512]{1,0:T(8,128)S(1)} %get-tuple-element.14), channel_id=1, source_target_pairs={{0,16},{8,24},{16,32},{24,40},{32,48},{40,56},{48,64},{56,72},{64,... | collective-permute-start | bytes 786440 | tf_op jit(solution)/shard_map/ppermute | solution.py:14
  91.5 145.8 %collective-permute-start.8 = (f32[128,512]{1,0:T(8,128)S(1)}, f32[128,512]{1,0:T(8,128)S(1)}, u32[]{:S(2)}, u32[]{:S(2)}) collective-permute-start(f32[128,512]{1,0:T(8,128)S(1)} %broadcast_select_fusion.13), channel_id=1, source_target_pairs={{0,32},{8,40},{16,48},{24,56},{32,64},{40,72},{48,80},{56,88},{64,... | collective-permute-start | bytes 786440 | tf_op jit(solution)/shard_map/ppermute | solution.py:14
  94.6 153.0 %collective-permute-start.2 = (f32[128,512]{1,0:T(8,128)S(1)}, f32[128,512]{1,0:T(8,128)S(1)}, u32[]{:S(2)}, u32[]{:S(2)}) collective-permute-start(f32[128,512]{1,0:T(8,128)S(1)} %broadcast_select_fusion.19), channel_id=1, source_target_pairs={{0,32},{8,40},{16,48},{24,56},{32,64},{40,72},{48,80},{56,88},{64,... | collective-permute-start | bytes 786440 | tf_op jit(solution)/shard_map/ppermute | solution.py:14
  209.4 43.9 %collective-permute-start.14 = (f32[128,512]{1,0:T(8,128)S(1)}, f32[128,512]{1,0:T(8,128)S(1)}, u32[]{:S(2)}, u32[]{:S(2)}) collective-permute-start(f32[128,512]{1,0:T(8,128)S(1)} %broadcast_select_fusion.7), channel_id=1, source_target_pairs={{0,32},{8,40},{16,48},{24,56},{32,64},{40,72},{48,80},{56,88},{64,... | collective-permute-start | bytes 786440 | tf_op jit(solution)/shard_map/ppermute | solution.py:14
  229.5 27.3 %collective-permute-start.20 = (f32[128,512]{1,0:T(8,128)S(1)}, f32[128,512]{1,0:T(8,128)S(1)}, u32[]{:S(2)}, u32[]{:S(2)}) collective-permute-start(f32[128,512]{1,0:T(8,128)S(1)} %broadcast_select_fusion.1), channel_id=1, source_target_pairs={{0,32},{8,40},{16,48},{24,56},{32,64},{40,72},{48,80},{56,88},{64,... | collective-permute-start | bytes 786440 | tf_op jit(solution)/shard_map/ppermute | solution.py:14
  237.4 28.5 %collective-permute-start.9 = (f32[128,512]{1,0:T(8,128)S(1)}, f32[128,512]{1,0:T(8,128)S(1)}, u32[]{:S(2)}, u32[]{:S(2)}) collective-permute-start(f32[128,512]{1,0:T(8,128)S(1)} %broadcast_select_fusion.14), channel_id=1, source_target_pairs={{0,64},{8,72},{16,80},{24,88},{32,96},{40,104},{48,112},{56,120},{... | collective-permute-start | bytes 786440 | tf_op jit(solution)/shard_map/ppermute | solution.py:14
  247.7 19.5 %collective-permute-start.3 = (f32[128,512]{1,0:T(8,128)S(1)}, f32[128,512]{1,0:T(8,128)S(1)}, u32[]{:S(2)}, u32[]{:S(2)}) collective-permute-start(f32[128,512]{1,0:T(8,128)S(1)} %broadcast_select_fusion.20), channel_id=1, source_target_pairs={{0,64},{8,72},{16,80},{24,88},{32,96},{40,104},{48,112},{56,120},{... | collective-permute-start | bytes 786440 | tf_op jit(solution)/shard_map/ppermute | solution.py:14
  253.4 15.2 %collective-permute-start.15 = (f32[128,512]{1,0:T(8,128)S(1)}, f32[128,512]{1,0:T(8,128)S(1)}, u32[]{:S(2)}, u32[]{:S(2)}) collective-permute-start(f32[128,512]{1,0:T(8,128)S(1)} %broadcast_select_fusion.8), channel_id=1, source_target_pairs={{0,64},{8,72},{16,80},{24,88},{32,96},{40,104},{48,112},{56,120},{... | collective-permute-start | bytes 786440 | tf_op jit(solution)/shard_map/ppermute | solution.py:14
  256.9 15.9 %collective-permute-start.21 = (f32[128,512]{1,0:T(8,128)S(1)}, f32[128,512]{1,0:T(8,128)S(1)}, u32[]{:S(2)}, u32[]{:S(2)}) collective-permute-start(f32[128,512]{1,0:T(8,128)S(1)} %broadcast_select_fusion.2), channel_id=1, source_target_pairs={{0,64},{8,72},{16,80},{24,88},{32,96},{40,104},{48,112},{56,120},{... | collective-permute-start | bytes 786440 | tf_op jit(solution)/shard_map/ppermute | solution.py:14
  265.9 14.9 %collective-permute-start.10 = (f32[128,512]{1,0:T(8,128)S(1)}, f32[128,512]{1,0:T(8,128)S(1)}, u32[]{:S(2)}, u32[]{:S(2)}) collective-permute-start(f32[128,512]{1,0:T(8,128)S(1)} %broadcast_select_fusion.15), channel_id=1, source_target_pairs={{0,128},{8,136},{16,144},{24,152},{32,160},{40,168},{48,176},{56,1... | collective-permute-start | bytes 786440 | tf_op jit(solution)/shard_map/ppermute | solution.py:14
  267.3 19.2 %collective-permute-start.4 = (f32[128,512]{1,0:T(8,128)S(1)}, f32[128,512]{1,0:T(8,128)S(1)}, u32[]{:S(2)}, u32[]{:S(2)}) collective-permute-start(f32[128,512]{1,0:T(8,128)S(1)} %broadcast_select_fusion.21), channel_id=1, source_target_pairs={{0,128},{8,136},{16,144},{24,152},{32,160},{40,168},{48,176},{56,1... | collective-permute-start | bytes 786440 | tf_op jit(solution)/shard_map/ppermute | solution.py:14
  268.6 23.4 %collective-permute-start.16 = (f32[128,512]{1,0:T(8,128)S(1)}, f32[128,512]{1,0:T(8,128)S(1)}, u32[]{:S(2)}, u32[]{:S(2)}) collective-permute-start(f32[128,512]{1,0:T(8,128)S(1)} %broadcast_select_fusion.9), channel_id=1, source_target_pairs={{0,128},{8,136},{16,144},{24,152},{32,160},{40,168},{48,176},{56,1... | collective-permute-start | bytes 786440 | tf_op jit(solution)/shard_map/ppermute | solution.py:14
  272.9 24.9 %collective-permute-start.22 = (f32[128,512]{1,0:T(8,128)S(1)}, f32[128,512]{1,0:T(8,128)S(1)}, u32[]{:S(2)}, u32[]{:S(2)}) collective-permute-start(f32[128,512]{1,0:T(8,128)S(1)} %broadcast_select_fusion.3), channel_id=1, source_target_pairs={{0,128},{8,136},{16,144},{24,152},{32,160},{40,168},{48,176},{56,1... | collective-permute-start | bytes 786440 | tf_op jit(solution)/shard_map/ppermute | solution.py:14
  280.9 22.5 %collective-permute-start.11 = (f32[128,512]{1,0:T(8,128)S(1)}, f32[128,512]{1,0:T(8,128)S(1)}, u32[]{:S(2)}, u32[]{:S(2)}) collective-permute-start(f32[128,512]{1,0:T(8,128)S(1)} %broadcast_select_fusion.16), channel_id=1, source_target_pairs={{0,256},{8,264},{16,272},{24,280},{32,288},{40,296},{48,304},{56,3... | collective-permute-start | bytes 786440 | tf_op jit(solution)/shard_map/ppermute | solution.py:14
  286.5 22.6 %collective-permute-start.5 = (f32[128,512]{1,0:T(8,128)S(1)}, f32[128,512]{1,0:T(8,128)S(1)}, u32[]{:S(2)}, u32[]{:S(2)}) collective-permute-start(f32[128,512]{1,0:T(8,128)S(1)} %broadcast_select_fusion.22), channel_id=1, source_target_pairs={{0,256},{8,264},{16,272},{24,280},{32,288},{40,296},{48,304},{56,3... | collective-permute-start | bytes 786440 | tf_op jit(solution)/shard_map/ppermute | solution.py:14
  292.1 23.1 %collective-permute-start.17 = (f32[128,512]{1,0:T(8,128)S(1)}, f32[128,512]{1,0:T(8,128)S(1)}, u32[]{:S(2)}, u32[]{:S(2)}) collective-permute-start(f32[128,512]{1,0:T(8,128)S(1)} %broadcast_select_fusion.10), channel_id=1, source_target_pairs={{0,256},{8,264},{16,272},{24,280},{32,288},{40,296},{48,304},{56,3... | collective-permute-start | bytes 786440 | tf_op jit(solution)/shard_map/ppermute | solution.py:14
  297.8 40.4 %collective-permute-start.23 = (f32[128,512]{1,0:T(8,128)S(1)}, f32[128,512]{1,0:T(8,128)S(1)}, u32[]{:S(2)}, u32[]{:S(2)}) collective-permute-start(f32[128,512]{1,0:T(8,128)S(1)} %broadcast_select_fusion.4), channel_id=1, source_target_pairs={{0,256},{8,264},{16,272},{24,280},{32,288},{40,296},{48,304},{56,3... | collective-permute-start | bytes 786440 | tf_op jit(solution)/shard_map/ppermute | solution.py:14
  303.4 38.1 %collective-permute-start.12 = (f32[128,512]{1,0:T(8,128)S(1)}, f32[128,512]{1,0:T(8,128)S(1)}, u32[]{:S(2)}, u32[]{:S(2)}) collective-permute-start(f32[128,512]{1,0:T(8,128)S(1)} %broadcast_select_fusion.17), channel_id=1, source_target_pairs={{0,8},{8,16},{16,24},{24,32},{32,40},{40,48},{48,56},{56,64},{64,7... | collective-permute-start | bytes 786440 | tf_op jit(solution)/shard_map/ppermute | solution.py:14
  309.7 33.0 %collective-permute-start.6 = (f32[128,512]{1,0:T(8,128)S(1)}, f32[128,512]{1,0:T(8,128)S(1)}, u32[]{:S(2)}, u32[]{:S(2)}) collective-permute-start(f32[128,512]{1,0:T(8,128)S(1)} %broadcast_select_fusion.23), channel_id=1, source_target_pairs={{0,8},{8,16},{16,24},{24,32},{32,40},{40,48},{48,56},{56,64},{64,7... | collective-permute-start | bytes 786440 | tf_op jit(solution)/shard_map/ppermute | solution.py:14
  315.8 29.7 %collective-permute-start.18 = (f32[128,512]{1,0:T(8,128)S(1)}, f32[128,512]{1,0:T(8,128)S(1)}, u32[]{:S(2)}, u32[]{:S(2)}) collective-permute-start(f32[128,512]{1,0:T(8,128)S(1)} %broadcast_select_fusion.11), channel_id=1, source_target_pairs={{0,8},{8,16},{16,24},{24,32},{32,40},{40,48},{48,56},{56,64},{64,7... | collective-permute-start | bytes 786440 | tf_op jit(solution)/shard_map/ppermute | solution.py:14
  338.8 9.5 %collective-permute-start.24 = (f32[128,512]{1,0:T(8,128)S(1)}, f32[128,512]{1,0:T(8,128)S(1)}, u32[]{:S(2)}, u32[]{:S(2)}) collective-permute-start(f32[128,512]{1,0:T(8,128)S(1)} %broadcast_select_fusion.5), channel_id=1, source_target_pairs={{0,8},{8,16},{16,24},{24,32},{32,40},{40,48},{48,56},{56,64},{64,7... | collective-permute-start | bytes 786440 | tf_op jit(solution)/shard_map/ppermute | solution.py:14
  443.8 3.7 copy-start.7
  452.5 1.7 copy-start.10
  454.5 1.8 copy-start.11
  456.5 1.8 copy-start.8
  458.5 1.8 copy-start.9
  470.9 1.8 copy-start.3
  470.9 1.8 copy-start.4
  470.9 1.8 copy-start.12
  472.7 1.0 copy-start
  472.7 1.2 copy-start.5
  472.8 1.3 copy-start.6
  474.6 1.0 copy-start.1
  474.6 1.2 copy-start.2
  474.6 1.7 copy-start.13
  474.6 1.7 copy-start.15
Sparse Core Ops, SparseCore 0:
  53.3 386.0 all-gather.1
where the time goes:
time: 492 us; the launch traced here: 484 us
  starting transfers between devices  252 us (51%)
  waiting for transfers between devices  109 us (22%)
  blocking collectives  40.3 us (8%)
  local copies, waits for them, and re-layouts  28.3 us (6%)
  matrix products  25.7 us (5%)
  between operations  25.4 us (5%)
    ppermute x25, starting transfers between devices, shifted(): return lax.ppermute(block, axis, route)  252 us
    all_gather x1, waiting for transfers between devices, local(): all_taps = lax.all_gather(run_taps, 'seq', axis=0, tiled=True)  88.3 us
    all_gather x1, blocking collectives, local(): run_taps = lax.all_gather(taps, 'chan', axis=0, tiled=True)  40.3 us
    dot_general x24, matrix products, exact_dot(): jnp.dot(left, right, precision=precise, preferred_element_type=jnp.float32)  20.9 us
    ppermute x25, waiting for transfers between devices, shifted(): return lax.ppermute(block, axis, route)  20.3 us
  transfers between devices with their start and end apart: 26, of which 7 were waited for; matrix products, arithmetic and copies ran while one was open for 4% of the time, Pallas kernels for 0%

commit v1 on v0

v1 whole, which is shorter than its diff:
```python
import functools

import jax
import jax.numpy as jnp
from jax import lax
from jax.experimental import pallas as pl
from jax.experimental.pallas import tpu as pltpu
from jax.sharding import PartitionSpec as P


def split(x):
    hi = x.astype(jnp.bfloat16)
    lo = (x - hi.astype(jnp.float32)).astype(jnp.bfloat16)
    return hi, lo


def dot(a, b):
    return jnp.dot(a, b, preferred_element_type=jnp.float32)


def conv_kernel(groups_ref, offsets_ref, x_ref, taps_ref, y_ref, padded, toep_hi, toep_lo):
    blocks, channels, width = x_ref.shape
    lags = taps_ref.shape[1]
    padded[:blocks] = jnp.zeros((blocks, width), jnp.float32)
    for c in range(channels):
        padded[blocks:] = x_ref[:, c, :]
        filt = taps_ref[groups_ref[c]]
        parts = []
        for k in range(lags):
            parts.append(padded[pl.ds(blocks - offsets_ref[k], blocks), :])
            row = jnp.concatenate([filt[k : k + 1], jnp.zeros((1, width), jnp.float32)], axis=1)
            rows = jnp.broadcast_to(row, (width, 2 * width))
            toep = pltpu.roll(rows, 0, 1, stride=1, stride_axis=0)
            hi, lo = split(toep)
            toep_hi[k * width : (k + 1) * width] = hi
            toep_lo[k * width : (k + 1) * width] = lo
        hi, lo = split(jnp.concatenate(parts, axis=1))
        y = dot(hi, toep_hi[...]) + dot(lo, toep_hi[...]) + dot(hi, toep_lo[...])
        tail = jnp.concatenate([jnp.zeros((1, width), jnp.float32), y[: blocks - 1, width:]], axis=0)
        y_ref[:, c, :] = y[:, :width] + tail


def convolve(x, taps, groups, offsets):
    lags, width = taps.shape[1:]
    smem = pl.BlockSpec(memory_space=pltpu.SMEM)
    vmem = pl.BlockSpec(memory_space=pltpu.VMEM)
    return pl.pallas_call(
        conv_kernel,
        out_shape=jax.ShapeDtypeStruct(x.shape, jnp.float32),
        in_specs=[smem, smem, vmem, vmem],
        out_specs=vmem,
        scratch_shapes=[
            pltpu.VMEM((2 * x.shape[0], width), jnp.float32),
            pltpu.VMEM((lags * width, 2 * width), jnp.bfloat16),
            pltpu.VMEM((lags * width, 2 * width), jnp.bfloat16),
        ],
    )(groups, offsets, x, taps)


def local(q_proj, k_proj, v_proj, taps, skip_bias, group_index, offsets):
    gated_in = k_proj * v_proj
    block_len, chans = gated_in.shape
    seq = lax.axis_size("seq")
    share = chans // seq
    run_taps = lax.all_gather(taps, "chan", axis=0, tiled=True)
    all_taps = lax.all_gather(run_taps, "seq", axis=0, tiled=True)
    sent = gated_in.T.reshape(seq, share, block_len)
    x = lax.all_to_all(sent, "seq", 0, 0, tiled=True)
    groups = lax.dynamic_slice(group_index, (lax.axis_index("seq") * share,), (share,))
    y = convolve(x, all_taps, groups, offsets)
    back = lax.all_to_all(y, "seq", 0, 0, tiled=True)
    convolved = back.reshape(chans, block_len).T
    return q_proj * (convolved + skip_bias[None, :] * gated_in)


def solution(mesh):
    return jax.shard_map(
        local,
        mesh=mesh,
        in_specs=(
            P("seq", "chan"),
            P("seq", "chan"),
            P("seq", "chan"),
            P(("seq", "chan"), None, None),
            P("chan"),
            P("chan"),
            P(),
        ),
        out_specs=P("seq", "chan"),
        check_vma=False,
    )
```

time: 492 us -> 201 us (0.41); the launches traced: 484 us -> 198 us
  starting transfers between devices: 252 us -> 24.1 us
  blocking collectives: 40.3 us -> 66.2 us
  matrix products: 25.7 us -> 0 us
  local copies, waits for them, and re-layouts: 28.3 us -> 3.13 us
  waiting for transfers between devices: 109 us -> 86 us
  between operations: 25.4 us -> 13.4 us
    ppermute x25 -> x0, starting transfers between devices: 252 us -> none  [shifted(): return lax.ppermute(block, axis, route)]
    dot_general x26 -> x0, matrix products: 25.7 us -> none  [the longest x24 20.9 us: exact_dot(): jnp.dot(left, right, precision=precise, preferred_element_type=jnp.float32)]
    all_to_all x0 -> x1, starting transfers between devices: none -> 24.1 us  [local(): x = lax.all_to_all(sent, 'seq', 0, 0, tiled=True)]
    all_to_all x0 -> x1, blocking collectives: none -> 23.8 us  [local(): back = lax.all_to_all(y, 'seq', 0, 0, tiled=True)]
    ppermute x25 -> x0, waiting for transfers between devices: 20.3 us -> none  [shifted(): return lax.ppermute(block, axis, route)]
    all_gather x1, waiting for transfers between devices: 88.3 us -> 68.3 us  [local(): all_taps = lax.all_gather(run_taps, 'seq', axis=0, tiled=True)]
    gather x16 -> x0, local copies, waits for them, and re-layouts: 18.6 us -> none  [the longest x8 9.63 us: local(): filt_re = jnp.take(tap_re[:, :, lag_index], group_index, axis=1)]
    all_to_all x0 -> x1, waiting for transfers between devices: none -> 17.6 us  [local(): x = lax.all_to_all(sent, 'seq', 0, 0, tiled=True)]
  transfers between devices with their start and end apart: 26 -> 2, of which waited for: 7 -> 2; matrix products, arithmetic and copies ran while one was open for 4% -> 2% of each run, Pallas kernels for 0% -> 0%
where the time goes in v1:
time: 201 us; the launch traced here: 198 us
  waiting for transfers between devices  86 us (43%)
  blocking collectives  66.2 us (33%)
  starting transfers between devices  24.1 us (12%)
  between operations  13.4 us (7%)
  Pallas kernels  3.63 us (2%)
  local copies, waits for them, and re-layouts  3.13 us (2%)
    all_gather x1, waiting for transfers between devices, local(): all_taps = lax.all_gather(run_taps, 'seq', axis=0, tiled=True)  68.3 us
    all_gather x1, blocking collectives, local(): run_taps = lax.all_gather(taps, 'chan', axis=0, tiled=True)  42.4 us
    all_to_all x1, starting transfers between devices, local(): x = lax.all_to_all(sent, 'seq', 0, 0, tiled=True)  24.1 us
    all_to_all x1, blocking collectives, local(): back = lax.all_to_all(y, 'seq', 0, 0, tiled=True)  23.8 us
    all_to_all x1, waiting for transfers between devices, local(): x = lax.all_to_all(sent, 'seq', 0, 0, tiled=True)  17.6 us
  transfers between devices with their start and end apart: 2, of which 2 were waited for; matrix products, arithmetic and copies ran while one was open for 2% of the time, Pallas kernels for 0%

profile of v1, /device:TPU:1, one launch (start us, length us, event | category | flops | bytes accessed | tf_op | source)
XLA Modules:
  0.0 198.4 jit_solution(1954712608655338487)
XLA Ops:
  6.5 0.0 all-gather.2.cloned.1.call-start
  6.5 42.4 %all_gather.6 = f32[8,4,128]{2,1,0:T(4,128)} all-gather(f32[1,4,128]{2,1,0:T(4,128)} %param.10), channel_id=1, replica_groups=mesh['seq'=64,'chan'=8] {'chan'}, dimensions={0}, use_global_device_ids=true | all-gather | bytes 18432 | tf_op jit(solution)/shard_map/all_gather | solution.py:65
  48.9 0.0 all-gather.2.cloned.1.call-update
  49.0 1.1 multiply_bitcast_fusion
  50.0 0.8 copy.10
  50.9 24.1 %all-to-all-start = ((f32[64,8,128]{2,1,0:T(8,128)}), f32[64,8,128]{2,1,0:T(8,128)S(1)}, u32[]{:S(2)}, u32[]{:S(2)}) async-start(f32[64,8,128]{2,1,0:T(8,128)} %bitcast.1), calls=%async_computation | async-start | bytes 524288 | tf_op jit(solution)/shard_map/all_to_all | solution.py:68
  75.0 1.3 dynamic_slice.3.groups_ref
  76.3 17.6 %all-to-all-done.x_ref = f32[64,8,128]{2,1,0:T(8,128)S(1)} async-done(((f32[64,8,128]{2,1,0:T(8,128)}), f32[64,8,128]{2,1,0:T(8,128)S(1)}, u32[]{:S(2)}, u32[]{:S(2)}) %all-to-all-start) | async-done | bytes 262176 | tf_op jit(solution)/shard_map/all_to_all | solution.py:68
  93.9 0.0 copy-start.2
  93.9 68.3 %all-gather.2.cloned.1.call-done.taps_ref = f32[512,4,128]{2,1,0:T(4,128)} async-done(((f32[8,4,128]{2,1,0:T(4,128)}), f32[512,4,128]{2,1,0:T(4,128)}) %all-gather.2.cloned.1.call-update) | async-done | bytes 1048592 | tf_op jit(solution)/shard_map/all_gather | solution.py:66
  162.2 0.0 copy-done.2
  162.3 3.6 %shard_map.73 = f32[64,8,128]{2,1,0:T(8,128)} custom-call(s32[8]{0:T(128)} %dynamic_slice.3.groups_ref, s32[4]{0:T(128)} %offsets_ref.1, f32[64,8,128]{2,1,0:T(8,128)} %copy-done.2, f32[512,4,128]{2,1,0:T(4,128)} %all-gather.2.cloned.1.call-done.taps_ref), custom_call_target="tpu_custom_call" | custom-call | tf_op jit(solution)/shard_map/pallas_call | solution.py:47
  165.9 0.0 copy-start.3
  165.9 0.0 copy-start.4
  165.9 23.8 %all_to_all.10 = f32[64,8,128]{2,1,0:T(8,128)S(1)} all-to-all(f32[64,8,128]{2,1,0:T(8,128)} %shard_map.73), channel_id=1, replica_groups=mesh['seq'=64,'chan'=8] {'seq'}, dimensions={0} | all-to-all | bytes 524288 | tf_op jit(solution)/shard_map/all_to_all | solution.py:71
  189.7 0.0 copy-start
  189.7 0.0 copy-start.1
  189.7 0.1 copy.11
  189.9 0.0 copy-done.3
  189.9 0.0 copy-done.4
  189.9 0.8 copy-done
  190.7 0.1 copy-done.1
  190.8 0.8 fusion
Async XLA Ops:
  6.5 155.7 %all-gather.2.cloned.1.call-start = ((), (), s32[]{:S(2)}) async-start(), calls=%async_computation.2 | async-start | bytes 1064960 | tf_op jit(solution)/shard_map/all_gather | solution.py:66
  50.9 43.1 %all-to-all-start = ((f32[64,8,128]{2,1,0:T(8,128)}), f32[64,8,128]{2,1,0:T(8,128)S(1)}, u32[]{:S(2)}, u32[]{:S(2)}) async-start(f32[64,8,128]{2,1,0:T(8,128)} %bitcast.1), calls=%async_computation | async-start | bytes 524288 | tf_op jit(solution)/shard_map/all_to_all | solution.py:68
  93.9 68.3 %copy-start.2 = (f32[64,8,128]{2,1,0:T(8,128)}, f32[64,8,128]{2,1,0:T(8,128)S(1)}, u32[]{:S(2)}) copy-start(f32[64,8,128]{2,1,0:T(8,128)S(1)} %all-to-all-done.x_ref) | copy-start | bytes 786436
  165.9 24.0 %copy-start.3 = (f32[128,512]{1,0:T(8,128)S(1)}, f32[128,512]{1,0:T(8,128)}, u32[]{:S(2)}) copy-start(f32[128,512]{1,0:T(8,128)} %param.7) | copy-start | bytes 786436
  165.9 24.0 %copy-start.4 = (f32[512]{0:T(512)S(1)}, f32[512]{0:T(512)}, u32[]{:S(2)}) copy-start(f32[512]{0:T(512)} %param.11) | copy-start | bytes 6148
  189.7 1.0 copy-start
  189.7 1.0 copy-start.1
Sparse Core Ops, SparseCore 0:
  49.1 113.1 all-gather.1

commit v2 on v1

v2 whole, which is shorter than its diff:
```python
import functools

import jax
import jax.numpy as jnp
from jax import lax
from jax.experimental import pallas as pl
from jax.experimental.pallas import tpu as pltpu
from jax.sharding import PartitionSpec as P

MESH = pl.DeviceIdType.MESH
SUBS = 2


def split(x):
    hi = x.astype(jnp.bfloat16)
    lo = (x - hi.astype(jnp.float32)).astype(jnp.bfloat16)
    return hi, lo


def dot(a, b):
    return jnp.dot(a, b, preferred_element_type=jnp.float32)


def kernel(
    groups_ref,
    offsets_ref,
    q_ref,
    k_ref,
    v_ref,
    bias_ref,
    taps_ref,
    o_ref,
    sent,
    tiles,
    ring,
    padded,
    toep_hi,
    toep_lo,
    result,
    returned,
    column,
    table,
    tile_send,
    tile_recv,
    ring_send,
    ring_recv,
    tap_send,
    tap_recv,
    table_send,
    table_recv,
    back_send,
    back_recv,
):
    width = k_ref.shape[0]
    lags = taps_ref.shape[1]
    plane = tiles.shape[0]
    depth = column.shape[0]
    inner = 8
    slabs = plane // inner
    hops = depth // 2
    blocks = 2 * plane
    s = lax.axis_index("seq")
    j = lax.axis_index("chan")
    half = (s // inner) % 2
    p = (s // (2 * inner)) * inner + s % inner
    z = half * hops + j

    def at_plane(i):
        other = (p + i) % plane
        return other, {"seq": (other // inner) * 2 * inner + half * inner + other % inner}

    def at_z(step):
        there = (z + step + depth) % depth
        return {"seq": s + inner * (there // hops - half), "chan": there % hops}

    barrier = pltpu.get_barrier_semaphore()

    def greet(i, carry):
        _, device = at_plane(i)
        pl.semaphore_signal(barrier, inc=1, device_id=device, device_id_type=MESH)
        return carry

    for step in (1, -1):
        pl.semaphore_signal(barrier, inc=1, device_id=at_z(step), device_id_type=MESH)
    lax.fori_loop(1, plane, greet, 0)

    column[z] = taps_ref[0]
    for i in range(slabs):
        cols = slice(i * 128, (i + 1) * 128)
        turned = (k_ref[:, cols] * v_ref[:, cols]).T
        sent[i * inner : (i + 1) * inner] = turned.reshape(inner, SUBS, 8, width)
    padded[:, :blocks] = jnp.zeros((padded.shape[0], blocks, width), jnp.float32)
    pl.semaphore_wait(barrier, plane - 1 + 2)

    def tile_copy(i):
        other, device = at_plane(i)
        return pltpu.make_async_remote_copy(
            src_ref=sent.at[other],
            dst_ref=tiles.at[p],
            send_sem=tile_send,
            recv_sem=tile_recv,
            device_id=device,
            device_id_type=MESH,
        )

    def table_copy(i):
        _, device = at_plane(i)
        return pltpu.make_async_remote_copy(
            src_ref=column,
            dst_ref=table.at[pl.ds(p * depth, depth)],
            send_sem=table_send,
            recv_sem=table_recv,
            device_id=device,
            device_id_type=MESH,
        )

    def back_copy(i, sub):
        other, device = at_plane(i)
        return pltpu.make_async_remote_copy(
            src_ref=result.at[other, sub],
            dst_ref=returned.at[p, sub],
            send_sem=back_send.at[sub],
            recv_sem=back_recv.at[sub],
            device_id=device,
            device_id_type=MESH,
        )

    def start_all(copy):
        def start(i, carry):
            copy(i).start()
            return carry

        lax.fori_loop(1, plane, start, 0)

    def wait_bytes(ref, sem):
        pltpu.make_async_copy(ref, ref, sem).wait()

    def tap_copy(hop, way):
        origin = (z - (hop - 1) * (1, -1)[way] + depth) % depth
        return pltpu.make_async_remote_copy(
            src_ref=column.at[origin],
            dst_ref=column.at[origin],
            send_sem=tap_send.at[way, hop - 1],
            recv_sem=tap_recv.at[way, hop - 1],
            device_id=at_z((1, -1)[way]),
            device_id_type=MESH,
        )

    def ring_copy(hop, way, sub):
        return pltpu.make_async_remote_copy(
            src_ref=ring.at[way, hop - 1, sub],
            dst_ref=ring.at[way, hop, sub],
            send_sem=ring_send.at[way, hop - 1, sub],
            recv_sem=ring_recv.at[way, hop - 1, sub],
            device_id=at_z((1, -1)[way]),
            device_id_type=MESH,
        )

    def tap_hop(hop):
        for way in (0, 1):
            if hop > 1 and hop - 1 <= hops - way:
                tap_copy(hop - 1, way).wait_recv()
            if hop <= hops - way:
                tap_copy(hop, way).start()

    def ring_hop(hop, sub):
        for way in (0, 1):
            ring_copy(hop - 1, way, sub).wait_recv()
            ring_copy(hop, way, sub).start()

    start_all(tile_copy)
    tiles[p] = sent[p]
    for hop in range(1, 5):
        tap_hop(hop)

    wait_bytes(tiles.at[pl.ds(0, plane - 1)], tile_recv)
    chans = padded.shape[0]
    for c in range(chans):
        sub, way, i = c // 8, (c % 8) // 4, c % 4
        x = tiles[:, sub, c % 8, :]
        ring[way, 0, sub, i] = x
        for m in range(slabs):
            padded[c, pl.ds(pl.multiple_of(blocks + m * 2 * inner + half * inner, 8), inner), :] = x[m * inner : (m + 1) * inner]
    for sub in range(SUBS):
        for way in (0, 1):
            ring_copy(1, way, sub).start()

    for hop in range(5, hops + 2):
        tap_hop(hop)
    start_all(table_copy)
    table[pl.ds(p * depth, depth)] = column[...]

    def ring_step(hop, carry):
        for sub in range(SUBS):
            ring_hop(hop, sub)
        return carry

    lax.fori_loop(2, hops - 1, ring_step, 0)

    def toeplitz(c, carry):
        group = groups_ref[p * chans + c]
        owner = group // hops
        row = ((owner // (2 * inner)) * inner + owner % inner) * depth + ((owner // inner) % 2) * hops + group % hops
        filt = table[row]
        for lag in range(lags):
            line = jnp.concatenate([filt[lag : lag + 1], jnp.zeros((1, width), jnp.float32)], axis=1)
            lines = jnp.broadcast_to(line, (width, 2 * width))
            hi, lo = split(pltpu.roll(lines, 0, 1, stride=1, stride_axis=0))
            toep_hi[c, lag * width : (lag + 1) * width] = hi
            toep_lo[c, lag * width : (lag + 1) * width] = lo
        return carry

    wait_bytes(table.at[pl.ds(0, (plane - 1) * depth)], table_recv)
    piece = chans // (2 * SUBS)
    for hop in (hops - 1, hops):
        for sub in range(SUBS):
            ring_hop(hop, sub)
            first = ((hop - hops + 1) * SUBS + sub) * piece
            lax.fori_loop(first, first + piece, toeplitz, 0)

    def convolve(c, carry):
        sub, way, i = c // 8, (c % 8) // 4, c % 4
        x = ring[way, hops, sub, i]
        for m in range(slabs):
            padded[c, pl.ds(pl.multiple_of(blocks + m * 2 * inner + (1 - half) * inner, 8), inner), :] = x[m * inner : (m + 1) * inner]
        parts = [padded[c, pl.ds(blocks - offsets_ref[lag], blocks), :] for lag in range(lags)]
        hi, lo = split(jnp.concatenate(parts, axis=1))
        y = dot(hi, toep_hi[c]) + dot(lo, toep_hi[c]) + dot(hi, toep_lo[c])
        tail = jnp.concatenate([jnp.zeros((1, width), jnp.float32), y[: blocks - 1, width:]], axis=0)
        total = y[:, :width] + tail
        for m in range(slabs):
            low = total[m * 2 * inner : m * 2 * inner + inner]
            high = total[m * 2 * inner + inner : (m + 1) * 2 * inner]
            result[m * inner : (m + 1) * inner, sub, c % 8, :] = jnp.where(half == 0, low, high)
        return carry

    for sub in range(SUBS):
        for way in (0, 1):
            ring_copy(hops, way, sub).wait_recv()
        lax.fori_loop(sub * 8, (sub + 1) * 8, convolve, 0)
        start_all(functools.partial(back_copy, sub=sub))
    returned[p] = result[p]

    def drain(hop, carry):
        for sub in range(SUBS):
            for way in (0, 1):
                ring_copy(hop, way, sub).wait_send()
        return carry

    lax.fori_loop(1, hops + 1, drain, 0)
    for way in (0, 1):
        for hop in range(1, hops + 1 - way):
            tap_copy(hop, way).wait_send()
    wait_bytes(sent.at[pl.ds(0, plane - 1)], tile_send)
    wait_bytes(table.at[pl.ds(0, (plane - 1) * depth)], table_send)
    for sub in range(SUBS):
        wait_bytes(result.at[pl.ds(0, plane - 1), 0], back_send.at[sub])
    for sub in range(SUBS):
        wait_bytes(returned.at[pl.ds(0, plane - 1), 0], back_recv.at[sub])
    for i in range(slabs):
        cols = slice(i * 128, (i + 1) * 128)
        convolved = returned[i * inner : (i + 1) * inner].reshape(128, width).T
        gated = k_ref[:, cols] * v_ref[:, cols]
        o_ref[:, cols] = q_ref[:, cols] * (convolved + bias_ref[:, cols] * gated)


def local(q_proj, k_proj, v_proj, taps, skip_bias, group_index, offsets):
    width, chans = k_proj.shape
    lags = taps.shape[1]
    seq = lax.axis_size("seq")
    chan = lax.axis_size("chan")
    plane, depth = seq // 2, 2 * chan
    share = chans // plane
    smem = pl.BlockSpec(memory_space=pltpu.SMEM)
    vmem = pl.BlockSpec(memory_space=pltpu.VMEM)
    f32, b16, dma = jnp.float32, jnp.bfloat16, pltpu.SemaphoreType.DMA
    return pl.pallas_call(
        kernel,
        out_shape=jax.ShapeDtypeStruct((width, chans), f32),
        in_specs=[smem, smem, vmem, vmem, vmem, vmem, vmem],
        out_specs=vmem,
        scratch_shapes=[
            pltpu.VMEM((plane, SUBS, 8, width), f32),
            pltpu.VMEM((plane, SUBS, 8, width), f32),
            pltpu.VMEM((2, chan + 1, SUBS, 4, plane, width), f32),
            pltpu.VMEM((share, 2 * seq, width), f32),
            pltpu.VMEM((share, lags * width, 2 * width), b16),
            pltpu.VMEM((share, lags * width, 2 * width), b16),
            pltpu.VMEM((plane, SUBS, 8, width), f32),
            pltpu.VMEM((plane, SUBS, 8, width), f32),
            pltpu.VMEM((depth, lags, width), f32),
            pltpu.VMEM((plane * depth, lags, width), f32),
            dma(()),
            dma(()),
            dma((2, chan, SUBS)),
            dma((2, chan, SUBS)),
            dma((2, chan)),
            dma((2, chan)),
            dma(()),
            dma(()),
            dma((SUBS,)),
            dma((SUBS,)),
        ],
        compiler_params=pltpu.CompilerParams(collective_id=0, has_side_effects=True, vmem_limit_bytes=60 << 20),
    )(group_index, offsets, q_proj, k_proj, v_proj, skip_bias[None, :], taps)


def solution(mesh):
    return jax.shard_map(
        local,
        mesh=mesh,
        in_specs=(
            P("seq", "chan"),
            P("seq", "chan"),
            P("seq", "chan"),
            P(("seq", "chan"), None, None),
            P("chan"),
            P("chan"),
            P(),
        ),
        out_specs=P("seq", "chan"),
        check_vma=False,
    )
```

time: 201 us -> 78.4 us (0.39); the launches traced: 198 us -> 78.2 us
  waiting for transfers between devices: 86 us -> 0 us
  Pallas kernels: 3.63 us -> 76.6 us
  blocking collectives: 66.2 us -> 0 us
  starting transfers between devices: 24.1 us -> 0 us
  between operations: 13.4 us -> 0.01 us
    pallas_call x1, Pallas kernels: 3.63 us -> 76.6 us  [local(): pl.pallas_call(kernel, out_shape=jax.ShapeDtypeStruct((width, chans), f32...]
    all_gather x1 -> x0, waiting for transfers between devices: 68.3 us -> none  [local(): all_taps = lax.all_gather(run_taps, 'seq', axis=0, tiled=True)]
    all_gather x1 -> x0, blocking collectives: 42.4 us -> none  [local(): run_taps = lax.all_gather(taps, 'chan', axis=0, tiled=True)]
    all_to_all x1 -> x0, starting transfers between devices: 24.1 us -> none  [local(): x = lax.all_to_all(sent, 'seq', 0, 0, tiled=True)]
    all_to_all x1 -> x0, blocking collectives: 23.8 us -> none  [local(): back = lax.all_to_all(y, 'seq', 0, 0, tiled=True)]
    all_to_all x1 -> x0, waiting for transfers between devices: 17.6 us -> none  [local(): x = lax.all_to_all(sent, 'seq', 0, 0, tiled=True)]
  transfers between devices with their start and end apart: 2 -> 0, of which waited for: 2 -> 0; matrix products, arithmetic and copies ran while one was open for 2% -> 0% of each run, Pallas kernels for 0% -> 0%
where the time goes in v2:
time: 78.4 us; the launch traced here: 78.2 us
  Pallas kernels  76.6 us (98%)
  local copies, waits for them, and re-layouts  1.67 us (2%)
    pallas_call x1, Pallas kernels, local(): pl.pallas_call(kernel, out_shape=jax.ShapeDtypeStruct((width, chans), f32...  76.6 us
    unnamed x1, local copies, waits for them, and re-layouts  1.67 us

profile of v2, /device:TPU:1, one launch (start us, length us, event | category | flops | bytes accessed | tf_op | source)
XLA Modules:
  0.0 78.2 jit_solution(441558511372370117)
XLA Ops:
  0.0 76.6 %shard_map.73 = f32[128,512]{1,0:T(8,128)} custom-call(s32[512]{0:T(512)} %groups_ref.1, s32[4]{0:T(128)} %offsets_ref.1, f32[128,512]{1,0:T(8,128)} %q_ref.1, f32[128,512]{1,0:T(8,128)} %k_ref.1, f32[128,512]{1,0:T(8,128)} %v_ref.1, f32[1,512]{1,0:T(1,128)} %bitcast.1, f32[1,4,128]{2,1,0:T(4,128)} %taps_ref.1), custom_call_target="tpu_custom_call" | custom-call | tf_op jit(solution)/shard_map/pallas_call | solution.py:277
  76.6 1.7 %copy.9 = f32[128,512]{1,0:T(8,128)} copy(f32[128,512]{1,0:T(8,128)} %shard_map.73) | data formatting | bytes 524288

commit v3 on v2

v3 whole, which is shorter than its diff:
```python
import functools

import jax
import jax.numpy as jnp
from jax import lax
from jax.experimental import pallas as pl
from jax.experimental.pallas import tpu as pltpu
from jax.sharding import PartitionSpec as P

MESH = pl.DeviceIdType.MESH
SUBS = 2
PIECES = 2


def split(x):
    hi = x.astype(jnp.bfloat16)
    lo = (x - hi.astype(jnp.float32)).astype(jnp.bfloat16)
    return hi, lo


def dot(a, b):
    return jnp.dot(a, b, preferred_element_type=jnp.float32)


def kernel(
    groups_ref,
    offsets_ref,
    q_hbm,
    k_hbm,
    v_hbm,
    bias_ref,
    taps_hbm,
    o_ref,
    q_ref,
    k_ref,
    v_ref,
    sent,
    tiles,
    raw,
    foreign,
    ring,
    padded,
    toep_hi,
    toep_lo,
    result,
    returned,
    column,
    table,
    load_sem,
    tile_send,
    tile_recv,
    raw_send,
    raw_recv,
    foreign_send,
    foreign_recv,
    ring_send,
    ring_recv,
    tap_send,
    tap_recv,
    table_send,
    table_recv,
    back_send,
    back_recv,
):
    width = k_ref.shape[0]
    lags = taps_hbm.shape[1]
    plane = tiles.shape[1]
    depth = column.shape[0]
    chans = padded.shape[0]
    inner = 8
    slabs = plane // inner
    hops = depth // 2
    blocks = 2 * plane
    early = hops + 1
    s = lax.axis_index("seq")
    j = lax.axis_index("chan")
    half = (s // inner) % 2
    p = (s // (2 * inner)) * inner + s % inner
    z = half * hops + j

    def at_plane(i):
        other = (p + i) % plane
        return other, {"seq": (other // inner) * 2 * inner + half * inner + other % inner}

    def at_z(step):
        there = (z + step + depth) % depth
        return {"seq": s + inner * (there // hops - half), "chan": there % hops}

    loads = [
        pltpu.make_async_copy(src, dst, load_sem.at[i])
        for i, (src, dst) in enumerate(((k_hbm, k_ref), (v_hbm, v_ref), (taps_hbm.at[0], column.at[0]), (q_hbm, q_ref)))
    ]
    for load in loads:
        load.start()
    barrier = pltpu.get_barrier_semaphore()

    def greet(i, carry):
        _, device = at_plane(i)
        pl.semaphore_signal(barrier, inc=1, device_id=device, device_id_type=MESH)
        return carry

    for step in (1, -1):
        pl.semaphore_signal(barrier, inc=1, device_id=at_z(step), device_id_type=MESH)
    lax.fori_loop(1, plane, greet, 0)

    for load in loads:
        load.wait()
    for i in range(slabs):
        cols = slice(i * 128, (i + 1) * 128)
        turned = (k_ref[:, cols] * v_ref[:, cols]).T.reshape(inner, SUBS, 8, width)
        for sub in range(SUBS):
            sent[sub, i * inner : (i + 1) * inner] = turned[:, sub]
    padded[:, :blocks] = jnp.zeros((chans, blocks, width), jnp.float32)
    pl.semaphore_wait(barrier, plane - 1 + 2)

    def plane_copy(i, src, dst, send_sem, recv_sem):
        return pltpu.make_async_remote_copy(
            src_ref=src,
            dst_ref=dst,
            send_sem=send_sem,
            recv_sem=recv_sem,
            device_id=at_plane(i)[1],
            device_id_type=MESH,
        )

    def z_copy(way, src, dst, send_sem, recv_sem):
        return pltpu.make_async_remote_copy(
            src_ref=src,
            dst_ref=dst,
            send_sem=send_sem,
            recv_sem=recv_sem,
            device_id=at_z((1, -1)[way]),
            device_id_type=MESH,
        )

    def tile_copy(i):
        return plane_copy(i, sent.at[:, at_plane(i)[0]], tiles.at[:, p], tile_send, tile_recv)

    def table_copy(i, part):
        first, size = ((0, early), (early, depth - early))[part]
        src, dst = column.at[pl.ds(first, size)], table.at[pl.ds(p * depth + first, size)]
        return plane_copy(i, src, dst, table_send.at[part], table_recv.at[part])

    def foreign_copy(i):
        other = at_plane(i)[0]
        src = raw.at[other // (plane // 2), hops - 1, other % (plane // 2)]
        return plane_copy(i, src, foreign.at[p], foreign_send, foreign_recv)

    def back_copy(i, sub):
        return plane_copy(i, result.at[sub, at_plane(i)[0]], returned.at[sub, p], back_send.at[sub], back_recv.at[sub])

    def start_all(copy):
        def start(i, carry):
            copy(i).start()
            return carry

        lax.fori_loop(1, plane, start, 0)

    def wait_bytes(ref, sem):
        pltpu.make_async_copy(ref, ref, sem).wait()

    def place(hop, way):
        return 2 * hop - 1 + way if hop else 0

    def tap_copy(hop, way):
        src, dst = column.at[place(hop - 1, way)], column.at[place(hop, way)]
        return z_copy(way, src, dst, tap_send.at[way, hop - 1], tap_recv.at[way, hop - 1])

    def raw_copy(hop, way, piece):
        size = plane // 2 // PIECES
        src = sent.at[0, pl.ds(way * (plane // 2) + piece * size, size)] if hop == 1 else raw.at[way, hop - 2, pl.ds(piece * size, size)]
        dst = raw.at[way, hop - 1, pl.ds(piece * size, size)]
        return z_copy(way, src, dst, raw_send.at[way, hop - 1, piece], raw_recv.at[way, hop - 1, piece])

    def ring_copy(hop, way, piece):
        src, dst = ring.at[way, hop - 1, piece], ring.at[way, hop, piece]
        return z_copy(way, src, dst, ring_send.at[way, hop - 1, piece], ring_recv.at[way, hop - 1, piece])

    def tap_hop(hop):
        for way in (0, 1):
            if 1 < hop <= hops + 1 - way:
                tap_copy(hop - 1, way).wait_recv()
            if hop <= hops - way:
                tap_copy(hop, way).start()

    def hop_pieces(copy, hop):
        for piece in range(PIECES):
            for way in (0, 1):
                if hop > 1:
                    copy(hop - 1, way, piece).wait_recv()
                if hop <= hops:
                    copy(hop, way, piece).start()

    def own_rows(c, x, side):
        for m in range(slabs):
            row = pl.multiple_of(blocks + m * 2 * inner + side * inner, 8)
            padded[c, pl.ds(row, inner), :] = x[m * inner : (m + 1) * inner]

    tap_hop(1)
    hop_pieces(raw_copy, 1)
    start_all(tile_copy)
    tiles[:, p] = sent[:, p]
    tap_hop(2)
    hop_pieces(raw_copy, 2)
    tap_hop(3)
    hop_pieces(raw_copy, 3)
    tap_hop(4)
    wait_bytes(tiles.at[:, pl.ds(0, plane - 1)], tile_recv)
    for cc in range(8):
        x = tiles[1, :, cc, :]
        ring[cc // 4, 0, cc % 4 // (4 // PIECES), cc % (4 // PIECES)] = x
        own_rows(8 + cc, x, half)
    hop_pieces(ring_copy, 1)
    tap_hop(5)
    hop_pieces(raw_copy, 4)
    start_all(functools.partial(table_copy, part=0))
    tap_hop(6)
    hop_pieces(ring_copy, 2)
    hop_pieces(raw_copy, 5)
    tap_hop(7)
    hop_pieces(ring_copy, 3)
    tap_hop(8)
    hop_pieces(raw_copy, 6)
    tap_hop(9)
    start_all(functools.partial(table_copy, part=1))
    hop_pieces(ring_copy, 4)
    table[pl.ds(p * depth, depth)] = column[...]
    for cc in range(8):
        own_rows(cc, tiles[0, :, cc, :], half)
    hop_pieces(raw_copy, 7)
    hop_pieces(ring_copy, 5)
    hop_pieces(raw_copy, 8)
    hop_pieces(ring_copy, 6)
    hop_pieces(raw_copy, 9)
    start_all(foreign_copy)
    foreign[p] = raw[p // (plane // 2), hops - 1, p % (plane // 2)]
    hop_pieces(ring_copy, 7)
    row_at = lax.broadcasted_iota(jnp.int32, (width, width), 0)
    col_at = lax.broadcasted_iota(jnp.int32, (width, width), 1)
    same = col_at >= row_at
    none = jnp.zeros((width, width), jnp.bfloat16)

    def toeplitz(c, carry):
        group = groups_ref[p * chans + c]
        owner = group // hops
        away = ((owner // inner) % 2 * hops + group % hops - z + depth) % depth
        slot = jnp.where(away < hops, 2 * away, 2 * (depth - away) - 1)
        filt = table[((owner // (2 * inner)) * inner + owner % inner) * depth + slot]
        for lag in range(lags):
            lines = jnp.broadcast_to(filt[lag : lag + 1], (width, width))
            rows = slice(lag * width, (lag + 1) * width)
            for part, held in zip(split(pltpu.roll(lines, 0, 1, stride=1, stride_axis=0)), (toep_hi, toep_lo)):
                held[c, rows, :width] = jnp.where(same, part, none)
                held[c, rows, width:] = jnp.where(same, none, part)
        return carry

    wait_bytes(table.at[pl.ds(0, (plane - 1) * early)], table_recv.at[0])
    wait_bytes(table.at[pl.ds(0, (plane - 1) * (depth - early))], table_recv.at[1])
    lax.fori_loop(0, 8, toeplitz, 0, unroll=4)
    hop_pieces(ring_copy, 8)
    lax.fori_loop(8, 16, toeplitz, 0, unroll=4)

    def convolve(c, x):
        own_rows(c, x, 1 - half)
        parts = [padded[c, pl.ds(blocks - offsets_ref[lag], blocks), :] for lag in range(lags)]
        hi, lo = split(jnp.concatenate(parts, axis=1))
        both = dot(jnp.concatenate([hi, lo], axis=0), toep_hi[c])
        y = both[:blocks] + both[blocks:] + dot(hi, toep_lo[c])
        tail = jnp.concatenate([jnp.zeros((1, width), jnp.float32), y[: blocks - 1, width:]], axis=0)
        total = y[:, :width] + tail
        for m in range(slabs):
            low = total[m * 2 * inner : m * 2 * inner + inner]
            high = total[m * 2 * inner + inner : (m + 1) * 2 * inner]
            result[c // 8, m * inner : (m + 1) * inner, c % 8, :] = jnp.where(half == 0, low, high)

    wait_bytes(foreign.at[pl.ds(0, plane - 1)], foreign_recv)
    for cc in range(8):
        convolve(cc, foreign[:, cc, :])
    start_all(functools.partial(back_copy, sub=0))
    returned[0, p] = result[0, p]
    for piece in range(PIECES):
        for way in (0, 1):
            ring_copy(hops, way, piece).wait_recv()
        size = 4 // PIECES
        for way in (0, 1):
            for i in range(size):
                convolve(8 + way * 4 + piece * size + i, ring[way, hops, piece, i])
    start_all(functools.partial(back_copy, sub=1))
    returned[1, p] = result[1, p]
    for hop in range(1, hops + 1):
        for way in (0, 1):
            for piece in range(PIECES):
                raw_copy(hop, way, piece).wait_send()
                ring_copy(hop, way, piece).wait_send()
            if hop <= hops - way:
                tap_copy(hop, way).wait_send()
    wait_bytes(sent.at[:, pl.ds(0, plane - 1)], tile_send)
    wait_bytes(foreign.at[pl.ds(0, plane - 1)], foreign_send)
    wait_bytes(table.at[pl.ds(0, (plane - 1) * early)], table_send.at[0])
    wait_bytes(table.at[pl.ds(0, (plane - 1) * (depth - early))], table_send.at[1])
    for sub in range(SUBS):
        wait_bytes(result.at[sub, pl.ds(0, plane - 1)], back_send.at[sub])
    for sub in range(SUBS):
        wait_bytes(returned.at[sub, pl.ds(0, plane - 1)], back_recv.at[sub])
    for i in range(slabs):
        cols = slice(i * 128, (i + 1) * 128)
        halves = [returned[sub, i * inner : (i + 1) * inner] for sub in range(SUBS)]
        convolved = jnp.stack(halves, axis=1).reshape(128, width).T
        gated = k_ref[:, cols] * v_ref[:, cols]
        o_ref[:, cols] = q_ref[:, cols] * (convolved + bias_ref[:, cols] * gated)


def local(q_proj, k_proj, v_proj, taps, skip_bias, group_index, offsets):
    width, chans = k_proj.shape
    lags = taps.shape[1]
    seq = lax.axis_size("seq")
    chan = lax.axis_size("chan")
    plane, depth = seq // 2, 2 * chan
    share = chans // plane
    smem = pl.BlockSpec(memory_space=pltpu.SMEM)
    vmem = pl.BlockSpec(memory_space=pltpu.VMEM)
    hbm = pl.BlockSpec(memory_space=pl.ANY)
    f32, b16, dma = jnp.float32, jnp.bfloat16, pltpu.SemaphoreType.DMA
    return pl.pallas_call(
        kernel,
        out_shape=jax.ShapeDtypeStruct((width, chans), f32),
        in_specs=[smem, smem, hbm, hbm, hbm, vmem, hbm],
        out_specs=vmem,
        scratch_shapes=[
            pltpu.VMEM((width, chans), f32),
            pltpu.VMEM((width, chans), f32),
            pltpu.VMEM((width, chans), f32),
            pltpu.VMEM((SUBS, plane, 8, width), f32),
            pltpu.VMEM((SUBS, plane, 8, width), f32),
            pltpu.VMEM((2, chan, plane // 2, 8, width), f32),
            pltpu.VMEM((plane, 8, width), f32),
            pltpu.VMEM((2, chan + 1, PIECES, 4 // PIECES, plane, width), f32),
            pltpu.VMEM((share, 2 * seq, width), f32),
            pltpu.VMEM((share, lags * width, 2 * width), b16),
            pltpu.VMEM((share, lags * width, 2 * width), b16),
            pltpu.VMEM((SUBS, plane, 8, width), f32),
            pltpu.VMEM((SUBS, plane, 8, width), f32),
            pltpu.VMEM((depth, lags, width), f32),
            pltpu.VMEM((plane * depth, lags, width), f32),
            dma((4,)),
            dma(()),
            dma(()),
            dma((2, chan, PIECES)),
            dma((2, chan, PIECES)),
            dma(()),
            dma(()),
            dma((2, chan, PIECES)),
            dma((2, chan, PIECES)),
            dma((2, chan)),
            dma((2, chan)),
            dma((2,)),
            dma((2,)),
            dma((SUBS,)),
            dma((SUBS,)),
        ],
        compiler_params=pltpu.CompilerParams(collective_id=0, has_side_effects=True, vmem_limit_bytes=60 << 20),
    )(group_index, offsets, q_proj, k_proj, v_proj, skip_bias[None, :], taps)


def solution(mesh):
    return jax.shard_map(
        local,
        mesh=mesh,
        in_specs=(
            P("seq", "chan"),
            P("seq", "chan"),
            P("seq", "chan"),
            P(("seq", "chan"), None, None),
            P("chan"),
            P("chan"),
            P(),
        ),
        out_specs=P("seq", "chan"),
        check_vma=False,
    )
```

time: 78.4 us -> 65.4 us (0.83)
  Pallas kernels: 76.6 us -> 63.5 us
    pallas_call x1, Pallas kernels: 76.6 us -> 63.5 us  [local(): pl.pallas_call(kernel, out_shape=jax.ShapeDtypeStruct((width, chans), f32...]
where the time goes in v3:
time: 65.4 us; the launch traced here: 65.2 us
  Pallas kernels  63.5 us (97%)
  local copies, waits for them, and re-layouts  1.67 us (3%)
    pallas_call x1, Pallas kernels, local(): pl.pallas_call(kernel, out_shape=jax.ShapeDtypeStruct((width, chans), f32...  63.5 us
    unnamed x1, local copies, waits for them, and re-layouts  1.67 us

profile of v3, /device:TPU:1, one launch (start us, length us, event | category | flops | bytes accessed | tf_op | source)
XLA Modules:
  0.0 65.2 jit_solution(5893169096221894237)
XLA Ops:
  0.0 63.5 %shard_map.73 = f32[128,512]{1,0:T(8,128)} custom-call(s32[512]{0:T(512)} %groups_ref.1, s32[4]{0:T(128)} %offsets_ref.1, f32[128,512]{1,0:T(8,128)} %q_hbm.1, f32[128,512]{1,0:T(8,128)} %k_hbm.1, f32[128,512]{1,0:T(8,128)} %v_hbm.1, f32[1,512]{1,0:T(1,128)} %bitcast.1, f32[1,4,128]{2,1,0:T(4,128)} %taps_hbm.1), custom_call_target="tpu_custom_call" | custom-call | tf_op jit(solution)/shard_map/pallas_call | solution.py:324
  63.5 1.7 %copy.9 = f32[128,512]{1,0:T(8,128)} copy(f32[128,512]{1,0:T(8,128)} %shard_map.73) | data formatting | bytes 524288

commit v4 on v1

v4 whole, which is shorter than its diff:
```python
import functools

import jax
import jax.numpy as jnp
from jax import lax
from jax.experimental import pallas as pl
from jax.experimental.pallas import tpu as pltpu
from jax.sharding import PartitionSpec as P

MESH = pl.DeviceIdType.MESH
RAW = 4
RAW_PIECES = 1
PIECES = 4
BATCHES = 4


def split(x):
    hi = x.astype(jnp.bfloat16)
    lo = (x - hi.astype(jnp.float32)).astype(jnp.bfloat16)
    return hi, lo


def dot(a, b):
    return jnp.dot(a, b, preferred_element_type=jnp.float32)


def kernel(
    groups_hbm,
    offsets_hbm,
    q_hbm,
    k_hbm,
    v_hbm,
    bias_hbm,
    taps_hbm,
    o_ref,
    groups_ref,
    offsets_ref,
    q_ref,
    k_ref,
    v_ref,
    bias_ref,
    sent,
    tiles,
    raw,
    foreign,
    mine,
    far,
    padded,
    toep_hi,
    toep_lo,
    result,
    returned,
    column,
    table,
    load_sem,
    tile_send,
    tile_recv,
    raw_send,
    raw_recv,
    foreign_send,
    foreign_recv,
    far_send,
    far_recv,
    tap_send,
    tap_recv,
    table_send,
    table_recv,
    own_sem,
    twin_send,
    twin_recv,
    back_send,
    back_recv,
):
    width = k_ref.shape[0]
    lags = taps_hbm.shape[1]
    plane = tiles.shape[0]
    depth = column.shape[0]
    chans = padded.shape[0]
    chips = plane // 2
    batch = chans // BATCHES
    size = (chans - RAW) // PIECES
    inner = 8
    slabs = plane // inner
    chan = depth // 2
    blocks = 2 * plane
    s = lax.axis_index("seq")
    j = lax.axis_index("chan")
    half = (s // inner) % 2
    p = (s // (2 * inner)) * inner + s % inner
    z = half * chan + j

    mine_x, mine_y, core = p // inner, p // 2 % (inner // 2), p % 2

    def at_plane(step):
        right, up, other = step
        x, there = (mine_x + right) % slabs, (mine_y + up) % (inner // 2) * 2 + (core + other) % 2
        return x * inner + there, {"seq": x * 2 * inner + half * inner + there}

    def at_z(step):
        there = (z + step) % depth
        return there, {"seq": s + inner * (there // chan - half), "chan": there % chan}

    near = (2, 1, 3, 0)
    chip_steps = sorted(((x, y) for x in near for y in near), key=lambda xy: min(xy[0], 4 - xy[0]) + min(xy[1], 4 - xy[1]), reverse=True)
    plane_steps = [(x, y, other) for x, y in chip_steps for other in (1, 0)][:-1]
    same_steps = [(x, y, 0) for x, y in chip_steps[:-1]]
    z_steps = sorted(range(1, depth), key=lambda step: min(step, depth - step), reverse=True)
    partner = {"seq": s + inner * (1 - 2 * half)}
    twin = {"seq": s + 1 - 2 * core}

    barrier = pltpu.get_barrier_semaphore()

    def greet(device):
        pl.semaphore_signal(barrier, inc=1, device_id=device, device_id_type=MESH)

    for step in z_steps:
        greet(at_z(step)[1])
    loads = [
        pltpu.make_async_copy(src, dst, load_sem.at[i])
        for i, (src, dst) in enumerate(
            (
                (k_hbm, k_ref),
                (v_hbm, v_ref),
                (taps_hbm.at[0], column.at[z]),
                (q_hbm, q_ref),
                (bias_hbm, bias_ref),
                (groups_hbm, groups_ref),
                (offsets_hbm, offsets_ref),
            )
        )
    ]
    for load in loads:
        load.start()
    for step in plane_steps:
        greet(at_plane(step)[1])

    for load in loads:
        load.wait()
    for i in range(slabs):
        cols = slice(i * 128, (i + 1) * 128)
        turned = (k_ref[:, cols] * v_ref[:, cols]).T
        sent[i * inner : (i + 1) * inner] = turned.reshape(inner, chans, width)
    padded[:, :blocks] = jnp.zeros((chans, blocks, width), jnp.float32)
    padded[:, 2 * blocks - inner :] = jnp.zeros((chans, 2 * inner, width), jnp.float32)
    pl.semaphore_wait(barrier, plane - 1 + depth - 1)

    def copy_to(device, src, dst, send_sem, recv_sem):
        return pltpu.make_async_remote_copy(
            src_ref=src, dst_ref=dst, send_sem=send_sem, recv_sem=recv_sem, device_id=device, device_id_type=MESH
        )

    def tile_copy(i):
        other, device = at_plane(i)
        return copy_to(device, sent.at[other], tiles.at[p], tile_send, tile_recv)

    def table_copy(i):
        return copy_to(at_plane(i)[1], column, table.at[p % 2, p // 2], table_send, table_recv)

    def twin_copy():
        return copy_to(twin, table.at[p % 2], table.at[p % 2], twin_send, twin_recv)

    def foreign_copy(i):
        other, device = at_plane(i)
        rows = pl.ds(0, RAW)
        return copy_to(device, raw.at[other, rows], foreign.at[p, rows], foreign_send, foreign_recv)

    def back_copy(i, sub):
        other, device = at_plane(i)
        rows = pl.ds(sub * batch, batch)
        return copy_to(device, result.at[other, rows], returned.at[p, rows], back_send.at[sub], back_recv.at[sub])

    def tap_copy(i):
        return copy_to(at_z(i)[1], column.at[z], column.at[z], tap_send, tap_recv)

    def raw_copy(piece):
        rows = pl.ds(piece * (plane // RAW_PIECES), plane // RAW_PIECES)
        lanes = pl.ds(0, RAW)
        return copy_to(partner, sent.at[rows, lanes], raw.at[rows, lanes], raw_send.at[piece], raw_recv.at[piece])

    def far_copy(piece, count):
        rows, cols = pl.ds(piece * size, size), pl.ds(0, count)
        return copy_to(partner, mine.at[rows, cols], far.at[rows, cols], far_send.at[piece], far_recv.at[piece])

    def by_half(low, high, act):
        @pl.when(half == 0)
        def _():
            act(low)

        @pl.when(half == 1)
        def _():
            act(high)

    most = plane - inner

    def start_all(copy, steps):
        for step in steps:
            copy(step).start()

    def wait_bytes(ref, sem):
        pltpu.make_async_copy(ref, ref, sem).wait()

    def rows_of(c, x, side, last=0):
        for m in range(slabs):
            row = pl.multiple_of(blocks + m * 2 * inner + side * inner + (m == slabs - 1) * last, 8)
            padded[c, pl.ds(row, inner), :] = x[m * inner : (m + 1) * inner]

    start_all(tap_copy, z_steps)
    start_all(tile_copy, plane_steps)
    for piece in range(RAW_PIECES):
        raw_copy(piece).start()
    tiles[p] = sent[p]
    wait_bytes(tiles.at[pl.ds(0, plane - 1)], tile_recv)
    for piece in range(PIECES):
        for i in range(piece * size, (piece + 1) * size):
            x = tiles[:, RAW + i, :]
            mine[i] = x
            rows_of(RAW + i, x, half)
        by_half(plane, most, lambda count: far_copy(piece, count).start())
    for c in range(RAW):
        rows_of(c, tiles[:, c, :], half)
    wait_bytes(column.at[pl.ds(0, depth - 1)], tap_recv)
    start_all(table_copy, same_steps)
    own = pltpu.make_async_copy(column, table.at[p % 2, p // 2], own_sem)
    own.start()
    for piece in range(RAW_PIECES):
        raw_copy(piece).wait_recv()
    start_all(foreign_copy, plane_steps)
    foreign[p] = raw[p]
    own.wait()
    wait_bytes(table.at[0, pl.ds(0, chips - 1)], table_recv)
    twin_copy().start()
    row_at = lax.broadcasted_iota(jnp.int32, (width, width), 0)
    col_at = lax.broadcasted_iota(jnp.int32, (width, width), 1)
    same = col_at >= row_at
    none = jnp.zeros((width, width), jnp.bfloat16)

    def toeplitz(c, carry):
        group = groups_ref[p * chans + c]
        owner = group // chan
        there = (owner // inner) % 2 * chan + group % chan
        filt = table[owner % 2, (owner // (2 * inner)) * (inner // 2) + owner % inner // 2, there]
        for lag in range(lags):
            lines = jnp.broadcast_to(filt[lag : lag + 1], (width, width))
            rows = slice(lag * width, (lag + 1) * width)
            for part, held in zip(split(pltpu.roll(lines, 0, 1, stride=1, stride_axis=0)), (toep_hi, toep_lo)):
                held[c, rows, :width] = jnp.where(same, part, none)
                held[c, rows, width:] = jnp.where(same, none, part)
        return carry

    wait_bytes(table.at[0], twin_recv)
    lax.fori_loop(0, chans, toeplitz, 0, unroll=4)

    def convolve(c, x):
        rows_of(c, x, 1 - half, (1 - half) * inner)
        parts = [padded[c, pl.ds(blocks - offsets_ref[lag], blocks), :] for lag in range(lags)]
        hi, lo = split(jnp.concatenate(parts, axis=1))
        both = dot(jnp.concatenate([hi, lo], axis=0), toep_hi[c])
        y = both[:blocks] + both[blocks:] + dot(hi, toep_lo[c])
        tail = jnp.concatenate([jnp.zeros((1, width), jnp.float32), y[: blocks - 1, width:]], axis=0)
        total = y[:, :width] + tail
        for m in range(slabs):
            low = total[m * 2 * inner : m * 2 * inner + inner]
            high = total[m * 2 * inner + inner : (m + 1) * 2 * inner]
            result[m * inner : (m + 1) * inner, c, :] = jnp.where(half == 0, low, high)

    wait_bytes(foreign.at[pl.ds(0, plane - 1), pl.ds(0, RAW)], foreign_recv)
    for c in range(RAW):
        convolve(c, foreign[:, c, :])
        if (c + 1) % batch == 0:
            start_all(functools.partial(back_copy, sub=c // batch), plane_steps)
    for piece in range(PIECES):
        by_half(most, plane, lambda count: far_copy(piece, count).wait_recv())
        for i in range(piece * size, (piece + 1) * size):
            convolve(RAW + i, far[i])
            if (RAW + i + 1) % batch == 0 and RAW + i + 1 < chans:
                start_all(functools.partial(back_copy, sub=(RAW + i) // batch), plane_steps)
    start_all(functools.partial(back_copy, sub=BATCHES - 1), plane_steps)
    returned[p] = result[p]
    for piece in range(RAW_PIECES):
        raw_copy(piece).wait_send()
    for piece in range(PIECES):
        by_half(plane, most, lambda count: far_copy(piece, count).wait_send())
    wait_bytes(column.at[pl.ds(0, depth - 1)], tap_send)
    wait_bytes(sent.at[pl.ds(0, plane - 1)], tile_send)
    wait_bytes(foreign.at[pl.ds(0, plane - 1), pl.ds(0, RAW)], foreign_send)
    wait_bytes(table.at[0, pl.ds(0, chips - 1)], table_send)
    wait_bytes(table.at[0], twin_send)
    for sub in range(BATCHES):
        wait_bytes(result.at[pl.ds(0, plane - 1), pl.ds(0, batch)], back_send.at[sub])
    for sub in range(BATCHES):
        wait_bytes(returned.at[pl.ds(0, plane - 1), pl.ds(0, batch)], back_recv.at[sub])
    for i in range(slabs):
        cols = slice(i * 128, (i + 1) * 128)
        convolved = returned[i * inner : (i + 1) * inner].reshape(128, width).T
        gated = k_ref[:, cols] * v_ref[:, cols]
        o_ref[:, cols] = q_ref[:, cols] * (convolved + bias_ref[:, cols] * gated)


def local(q_proj, k_proj, v_proj, taps, skip_bias, group_index, offsets):
    width, chans = k_proj.shape
    lags = taps.shape[1]
    seq = lax.axis_size("seq")
    chan = lax.axis_size("chan")
    plane, depth = seq // 2, 2 * chan
    share = chans // plane
    hbm = pl.BlockSpec(memory_space=pltpu.HBM)
    f32, b16, dma = jnp.float32, jnp.bfloat16, pltpu.SemaphoreType.DMA
    return pl.pallas_call(
        kernel,
        out_shape=pltpu.VMEM((width, chans), f32),
        in_specs=[hbm] * 7,
        out_specs=pl.BlockSpec(memory_space=pltpu.VMEM),
        scratch_shapes=[
            pltpu.SMEM((chans,), jnp.int32),
            pltpu.SMEM((lags,), jnp.int32),
            pltpu.VMEM((width, chans), f32),
            pltpu.VMEM((width, chans), f32),
            pltpu.VMEM((width, chans), f32),
            pltpu.VMEM((1, chans), f32),
            pltpu.VMEM((plane, share, width), f32),
            pltpu.VMEM((plane, share, width), f32),
            pltpu.VMEM((plane, 8, width), f32),
            pltpu.VMEM((plane, 8, width), f32),
            pltpu.VMEM((share - RAW, plane, width), f32),
            pltpu.VMEM((share - RAW, plane, width), f32),
            pltpu.VMEM((share, 2 * seq + 8, width), f32),
            pltpu.VMEM((share, lags * width, 2 * width), b16),
            pltpu.VMEM((share, lags * width, 2 * width), b16),
            pltpu.VMEM((plane, share, width), f32),
            pltpu.VMEM((plane, share, width), f32),
            pltpu.VMEM((depth, lags, width), f32),
            pltpu.VMEM((2, plane // 2, depth, lags, width), f32),
            dma((7,)),
            dma(()),
            dma(()),
            dma((RAW_PIECES,)),
            dma((RAW_PIECES,)),
            dma(()),
            dma(()),
            dma((PIECES,)),
            dma((PIECES,)),
            dma(()),
            dma(()),
            dma(()),
            dma(()),
            dma(()),
            dma(()),
            dma(()),
            dma((BATCHES,)),
            dma((BATCHES,)),
        ],
        compiler_params=pltpu.CompilerParams(collective_id=0, has_side_effects=True, vmem_limit_bytes=58 << 20),
    )(group_index, offsets, q_proj, k_proj, v_proj, skip_bias[None, :], taps)


def solution(mesh):
    return jax.shard_map(
        local,
        mesh=mesh,
        in_specs=(
            P("seq", "chan"),
            P("seq", "chan"),
            P("seq", "chan"),
            P(("seq", "chan"), None, None),
            P("chan"),
            P("chan"),
            P(),
        ),
        out_specs=P("seq", "chan"),
        check_vma=False,
    )
```

time: 201 us -> 49.5 us (0.25); the launches traced: 198 us -> 49.3 us
  waiting for transfers between devices: 86 us -> 0 us
  blocking collectives: 66.2 us -> 0 us
  Pallas kernels: 3.63 us -> 48.6 us
  starting transfers between devices: 24.1 us -> 0 us
  between operations: 13.4 us -> 0.01 us
  local copies, waits for them, and re-layouts: 3.13 us -> 0.71 us
    all_gather x1 -> x0, waiting for transfers between devices: 68.3 us -> none  [local(): all_taps = lax.all_gather(run_taps, 'seq', axis=0, tiled=True)]
    pallas_call x1, Pallas kernels: 3.63 us -> 48.6 us  [local(): pl.pallas_call(kernel, out_shape=pltpu.VMEM((width, chans), f32), in_spec...]
    all_gather x1 -> x0, blocking collectives: 42.4 us -> none  [local(): run_taps = lax.all_gather(taps, 'chan', axis=0, tiled=True)]
    all_to_all x1 -> x0, starting transfers between devices: 24.1 us -> none  [local(): x = lax.all_to_all(sent, 'seq', 0, 0, tiled=True)]
    all_to_all x1 -> x0, blocking collectives: 23.8 us -> none  [local(): back = lax.all_to_all(y, 'seq', 0, 0, tiled=True)]
    all_to_all x1 -> x0, waiting for transfers between devices: 17.6 us -> none  [local(): x = lax.all_to_all(sent, 'seq', 0, 0, tiled=True)]
  transfers between devices with their start and end apart: 2 -> 0, of which waited for: 2 -> 0; matrix products, arithmetic and copies ran while one was open for 2% -> 0% of each run, Pallas kernels for 0% -> 0%
where the time goes in v4:
time: 49.5 us; the launch traced here: 49.3 us
  Pallas kernels  48.6 us (98%)
  local copies, waits for them, and re-layouts  0.71 us (1%)
    pallas_call x1, Pallas kernels, local(): pl.pallas_call(kernel, out_shape=pltpu.VMEM((width, chans), f32), in_spec...  48.6 us

profile of v4, /device:TPU:1, one launch (start us, length us, event | category | flops | bytes accessed | tf_op | source)
XLA Modules:
  0.0 49.3 jit_solution(16240251716149720654)
XLA Ops:
  0.0 48.6 %shard_map.73 = f32[128,512]{1,0:T(8,128)S(1)} custom-call(s32[512]{0:T(512)} %groups_hbm.1, s32[4]{0:T(128)} %offsets_hbm.1, f32[128,512]{1,0:T(8,128)} %q_hbm.1, f32[128,512]{1,0:T(8,128)} %k_hbm.1, f32[128,512]{1,0:T(8,128)} %v_hbm.1, f32[1,512]{1,0:T(1,128)} %bitcast.1, f32[1,4,128]{2,1,0:T(4,128)} %taps_hbm.1), custom_call_target="tpu_custom_call" | custom-call | tf_op jit(solution)/shard_map/pallas_call | solution.py:308
  48.6 0.7 %copy.9 = f32[128,512]{1,0:T(8,128)} copy(f32[128,512]{1,0:T(8,128)S(1)} %shard_map.73) | data formatting | bytes 524288

commit v5 on v4

--- a/solution.py
+++ b/solution.py
@@ -215,13 +215,23 @@
             x = tiles[:, RAW + i, :]
             mine[i] = x
             rows_of(RAW + i, x, half)
-        by_half(plane, most, lambda count: far_copy(piece, count).start())
+
+        @pl.when(half == 1)
+        def _():
+            far_copy(piece, most).start()
+
     for c in range(RAW):
         rows_of(c, tiles[:, c, :], half)
     wait_bytes(column.at[pl.ds(0, depth - 1)], tap_recv)
     start_all(table_copy, same_steps)
     own = pltpu.make_async_copy(column, table.at[p % 2, p // 2], own_sem)
     own.start()
+
+    @pl.when(half == 0)
+    def _():
+        for piece in range(PIECES):
+            far_copy(piece, plane).start()
+
     for piece in range(RAW_PIECES):
         raw_copy(piece).wait_recv()
     start_all(foreign_copy, plane_steps)

time: 49.5 us -> 46.3 us (0.935)
  Pallas kernels: 48.6 us -> 45.4 us
    pallas_call x1, Pallas kernels: 48.6 us -> 45.4 us  [local(): pl.pallas_call(kernel, out_shape=pltpu.VMEM((width, chans), f32), in_spec...]
where the time goes in v5:
time: 46.3 us; the launch traced here: 46.1 us
  Pallas kernels  45.4 us (98%)
  local copies, waits for them, and re-layouts  0.71 us (2%)
    pallas_call x1, Pallas kernels, local(): pl.pallas_call(kernel, out_shape=pltpu.VMEM((width, chans), f32), in_spec...  45.4 us

profile of v5, /device:TPU:1, one launch (start us, length us, event | category | flops | bytes accessed | tf_op | source)
XLA Modules:
  0.0 46.1 jit_solution(7349208937404115347)
XLA Ops:
  0.0 45.4 %shard_map.73 = f32[128,512]{1,0:T(8,128)S(1)} custom-call(s32[512]{0:T(512)} %groups_hbm.1, s32[4]{0:T(128)} %offsets_hbm.1, f32[128,512]{1,0:T(8,128)} %q_hbm.1, f32[128,512]{1,0:T(8,128)} %k_hbm.1, f32[128,512]{1,0:T(8,128)} %v_hbm.1, f32[1,512]{1,0:T(1,128)} %bitcast.1, f32[1,4,128]{2,1,0:T(4,128)} %taps_hbm.1), custom_call_target="tpu_custom_call" | custom-call | tf_op jit(solution)/shard_map/pallas_call | solution.py:318
  45.4 0.7 %copy.9 = f32[128,512]{1,0:T(8,128)} copy(f32[128,512]{1,0:T(8,128)S(1)} %shard_map.73) | data formatting | bytes 524288

commit v6 on v5

--- a/solution.py
+++ b/solution.py
@@ -10,7 +10,7 @@
 MESH = pl.DeviceIdType.MESH
 RAW = 4
 RAW_PIECES = 1
-PIECES = 4
+PIECES = 6
 BATCHES = 4
 
 
@@ -273,17 +273,20 @@
             high = total[m * 2 * inner + inner : (m + 1) * 2 * inner]
             result[m * inner : (m + 1) * inner, c, :] = jnp.where(half == 0, low, high)
 
-    wait_bytes(foreign.at[pl.ds(0, plane - 1), pl.ds(0, RAW)], foreign_recv)
-    for c in range(RAW):
-        convolve(c, foreign[:, c, :])
-        if (c + 1) % batch == 0:
+    def give_back(c):
+        if (c + 1) % batch == 0 and c + 1 < chans:
             start_all(functools.partial(back_copy, sub=c // batch), plane_steps)
+
     for piece in range(PIECES):
+        if piece == 4:
+            wait_bytes(foreign.at[pl.ds(0, plane - 1), pl.ds(0, RAW)], foreign_recv)
+            for c in range(RAW):
+                convolve(c, foreign[:, c, :])
+                give_back(c)
         by_half(most, plane, lambda count: far_copy(piece, count).wait_recv())
-        for i in range(piece * size, (piece + 1) * size):
-            convolve(RAW + i, far[i])
-            if (RAW + i + 1) % batch == 0 and RAW + i + 1 < chans:
-                start_all(functools.partial(back_copy, sub=(RAW + i) // batch), plane_steps)
+        for c in range(RAW + piece * size, RAW + (piece + 1) * size):
+            convolve(c, far[c - RAW])
+            give_back(c)
     start_all(functools.partial(back_copy, sub=BATCHES - 1), plane_steps)
     returned[p] = result[p]
     for piece in range(RAW_PIECES):

time: 46.3 us -> 46.2 us (level)
  no operation moved by 1% of the time
where the time goes in v6:
time: 46.2 us; the launch traced here: 46 us
  Pallas kernels  45.3 us (98%)
  local copies, waits for them, and re-layouts  0.71 us (2%)
    pallas_call x1, Pallas kernels, local(): pl.pallas_call(kernel, out_shape=pltpu.VMEM((width, chans), f32), in_spec...  45.3 us

profile of v6, /device:TPU:1, one launch (start us, length us, event | category | flops | bytes accessed | tf_op | source)
XLA Modules:
  0.0 46.0 jit_solution(6362289442528020948)
XLA Ops:
  0.0 45.3 %shard_map.73 = f32[128,512]{1,0:T(8,128)S(1)} custom-call(s32[512]{0:T(512)} %groups_hbm.1, s32[4]{0:T(128)} %offsets_hbm.1, f32[128,512]{1,0:T(8,128)} %q_hbm.1, f32[128,512]{1,0:T(8,128)} %k_hbm.1, f32[128,512]{1,0:T(8,128)} %v_hbm.1, f32[1,512]{1,0:T(1,128)} %bitcast.1, f32[1,4,128]{2,1,0:T(4,128)} %taps_hbm.1), custom_call_target="tpu_custom_call" | custom-call | tf_op jit(solution)/shard_map/pallas_call | solution.py:321
  45.3 0.7 %copy.9 = f32[128,512]{1,0:T(8,128)} copy(f32[128,512]{1,0:T(8,128)S(1)} %shard_map.73) | data formatting | bytes 524288
